TPU v7x, 256 devices: a whole 4x4x8 slice. The times are simulated.
256 devices in a mesh: pipe: 4 (over x), seq: 64 (over y, z, core).
Axes of the slice: x: 4, y: 4, z: 8, core: 2. Of those that a mesh axis runs over, the one named last changes fastest.
Arguments:
- arriving: bfloat16 [4, 65536, 2048], P('pipe', 'seq'), may hold values from -6 to 6
- loss_grad: bfloat16 [65536, 2048], P('seq', 'pipe'), may hold values from -6 to 6
- first_blocks: bfloat16 [4, 256, 256, 256], P('pipe', 'seq'), may hold values from -0.375 to 0.375
- second_blocks: bfloat16 [4, 256, 256, 256], P('pipe', 'seq'), may hold values from -0.375 to 0.375
- inner_gain: bfloat16 [4, 2048], P('pipe'), may hold values from 0.25 to 1.75
- outer_gain: bfloat16 [4, 2048], P('pipe'), may hold values from 0.25 to 1.75
Outputs:
- entering: bfloat16 [4, 65536, 2048], P('pipe', 'seq')
- leaving: bfloat16 [65536, 2048], P('seq', 'pipe')
All inputs are finite; a program needn't handle non-finite values.
Results may differ from a plain program's by a relative error of at most 0.0059.
Values may be sent and summed in bfloat16 or wider, within the bound.
No kernel may reach another device: no remote copies, remote signals or barrier semaphores. Data moves between devices by JAX's collectives and lax.ppermute only.
A program may use at most 128 MiB of HBM per device.

v0:
```python
import jax
import jax.numpy as jnp
from jax import lax
from jax.sharding import PartitionSpec as P


def shifted(block, axis, distance):
    devices = range(lax.axis_size(axis))
    route = [((i - distance) % len(devices), i) for i in devices]
    return lax.ppermute(block, axis, route)


def from_root(array, axis, root):
    mine = lax.axis_index(axis) == root
    return lax.psum(jnp.where(mine, array, jnp.zeros_like(array)), axis)


def mixer(gradient, first_part, second_part, inner_part, outer_part):
    row_count = first_part.shape[0]
    block_order = first_part.shape[1]
    blocked = gradient.reshape(row_count, block_order, gradient.shape[1]).astype(jnp.float32)
    scaled = (blocked * inner_part.astype(jnp.float32)).astype(jnp.bfloat16)
    mixed = jnp.einsum(
        "kjc,jki->ijc",
        lax.all_to_all(scaled, "seq", split_axis=1, concat_axis=0, tiled=True),
        second_part,
        preferred_element_type=jnp.float32,
    ).astype(jnp.bfloat16)
    returned = lax.all_to_all(mixed, "seq", split_axis=0, concat_axis=1, tiled=True)
    spread = jnp.einsum("ikc,ikj->ijc", returned, first_part, preferred_element_type=jnp.float32)
    result = blocked + outer_part.astype(jnp.float32) * spread
    return result.astype(jnp.bfloat16).reshape(gradient.shape)


def per_device(arriving, loss_grad, first_blocks, second_blocks, inner_gain, outer_gain):
    sections = lax.axis_size("pipe")
    position = lax.axis_index("pipe")
    whole_loss = lax.all_gather(loss_grad, "pipe", axis=1, tiled=True)
    own_result = mixer(arriving[0], first_blocks[0], second_blocks[0], inner_gain[0], outer_gain[0])
    passed = shifted(own_result, "pipe", -1)
    exit_root = sections - 1
    source = jnp.where(position == sections - 1, whole_loss, passed)
    entering = mixer(source, first_blocks[0], second_blocks[0], inner_gain[0], outer_gain[0])
    copied = from_root(passed, "pipe", exit_root)
    channel_width = loss_grad.shape[1]
    leaving = lax.dynamic_slice_in_dim(copied, position * channel_width, channel_width, 1)
    return (entering[None], leaving)


def solution(mesh):
    placed = (
        P("pipe", "seq", None),
        P("seq", "pipe"),
        P("pipe", "seq", None, None),
        P("pipe", "seq", None, None),
        P("pipe", None),
        P("pipe", None),
    )
    return jax.shard_map(
        per_device,
        mesh=mesh,
        in_specs=placed,
        out_specs=(P("pipe", "seq", None), P("seq", "pipe")),
        check_vma=False,
    )
```

profile of v0, /device:TPU:1, one launch (start us, length us, event | category | flops | bytes accessed | tf_op | source)
XLA Modules:
  0.0 639.2 jit_solution(10214228244827802752)
XLA Ops:
  7.2 0.0 copy-start
  7.2 0.8 convert_element_type.76
  7.9 3.3 fusion
  11.2 3.2 copy.24
  14.5 109.1 %all_to_all.72 = bf16[4,256,2048]{2,0,1:T(4,128)(2,1)S(1)} all-to-all(bf16[4,256,2048]{2,0,1:T(4,128)(2,1)S(1)} %copy.24), channel_id=1, replica_groups=mesh['pipe'=4,'seq'=64] {'seq'}, dimensions={1} | all-to-all | bytes 8388608 | tf_op jit(solution)/shard_map/all_to_all | solution.py:25
  123.6 8.3 %copy.25 = bf16[4,64,4,2048]{3,2,0,1:T(4,128)(2,1)S(1)} copy(bf16[4,64,4,2048]{3,0,2,1:T(4,128)(2,1)S(1)} %bitcast.44) | data formatting | bytes 8388608 | tf_op jit(solution)/shard_map/all_to_all | solution.py:25
  131.9 0.0 copy-done
  131.9 7.7 %convert_bitcast_fusion.1 = bf16[256,4,2048]{0,2,1:T(8,128)(2,1)} fusion(bf16[256,4,2048]{2,1,0:T(4,128)(2,1)S(1)} %bitcast.45, bf16[1,4,256,256]{3,2,1,0:T(8,128)(2,1)S(1)} %copy-done), kind=kOutput, calls=%fused_computation.13 | convolution fusion | flops 1075838976 | bytes 8912896 | tf_op jit(solution)/shard_map/kjc,jki->ijc/dot_general | solution.py:23
  139.6 7.9 %copy.27 = bf16[256,4,2048]{2,1,0:T(4,128)(2,1)} copy(bf16[256,4,2048]{0,2,1:T(8,128)(2,1)} %convert_bitcast_fusion.1) | data formatting | bytes 8388608 | tf_op jit(solution)/shard_map/convert_element_type | solution.py:28
  147.5 0.0 copy-start.3
  147.5 6.2 all-to-all-start.1
  153.7 0.0 all-gather.2.cloned.1.call-start
  153.7 0.7 all-gather.2.cloned.1.call-update
  154.4 0.0 copy-done.3
  154.4 95.1 %all-to-all-done.1 = bf16[256,4,2048]{2,1,0:T(4,128)(2,1)} async-done(((bf16[256,4,2048]{2,1,0:T(4,128)(2,1)}), bf16[256,4,2048]{2,1,0:T(4,128)(2,1)}, u32[]{:S(2)}, u32[]{:S(2)}) %all-to-all-start.1) | async-done | bytes 4194336 | tf_op jit(solution)/shard_map/all_to_all | solution.py:29
  249.5 7.0 %copy.28 = bf16[4,64,4,2048]{3,2,1,0:T(4,128)(2,1)} copy(bf16[4,64,4,2048]{3,2,0,1:T(4,128)(2,1)} %bitcast.10) | data formatting | bytes 8388608 | tf_op jit(solution)/shard_map/all_to_all | solution.py:29
  256.5 0.0 copy-start.2
  256.5 7.0 %all_to_all.59 = bf16[4,256,2048]{2,1,0:T(8,128)(2,1)} reshape(bf16[4,64,4,2048]{3,2,1,0:T(4,128)(2,1)} %copy.28) | data formatting | bytes 8388608 | tf_op jit(solution)/shard_map/all_to_all | solution.py:29
  263.5 0.0 copy-done.2
  263.5 6.9 %fusion.1 = bf16[4,256,2048]{2,1,0:T(8,128)(2,1)} fusion(bf16[4,256,2048]{2,1,0:T(8,128)(2,1)} %bitcast.49, bf16[4,256,2048]{2,1,0:T(8,128)(2,1)} %all_to_all.59, f32[2048]{0:T(1024)S(1)} %bitcast.53, bf16[1,4,256,256]{3,2,1,0:T(8,128)(2,1)S(1)} %copy-done.2), kind=kOutput, calls=%fused_computation.5 | convolution fusion | flops 1082130432 | bytes 13115392 | tf_op jit(solution)/shard_map/ikc,ikj->ijc/dot_general | solution.py:30
  270.5 2.5 collective-permute-start
  272.9 0.0 all-gather.2.cloned.1.call-done
  273.0 90.0 %collective-permute-done = bf16[1024,2048]{1,0:T(8,128)(2,1)} collective-permute-done((bf16[1024,2048]{1,0:T(8,128)(2,1)}, bf16[1024,2048]{1,0:T(8,128)(2,1)}, u32[]{:S(2)}, u32[]{:S(2)}) %collective-permute-start) | collective-permute-done | bytes 4194336 | tf_op jit(solution)/shard_map/ppermute | solution.py:10
  362.9 3.9 broadcast_select_fusion
  366.8 0.0 copy-start.1
  366.8 1.9 copy-done.1
  368.8 1.2 fusion.2
  369.9 3.2 copy.30
  373.2 101.9 %all_to_all.73 = bf16[4,256,2048]{2,0,1:T(4,128)(2,1)S(1)} all-to-all(bf16[4,256,2048]{2,0,1:T(4,128)(2,1)S(1)} %copy.30), channel_id=1, replica_groups=mesh['pipe'=4,'seq'=64] {'seq'}, dimensions={1} | all-to-all | bytes 8388608 | tf_op jit(solution)/shard_map/all_to_all | solution.py:25
  475.1 8.3 %copy.31 = bf16[4,64,4,2048]{3,2,0,1:T(4,128)(2,1)S(1)} copy(bf16[4,64,4,2048]{3,0,2,1:T(4,128)(2,1)S(1)} %bitcast.46) | data formatting | bytes 8388608 | tf_op jit(solution)/shard_map/all_to_all | solution.py:25
  483.4 7.5 %convert_bitcast_fusion = bf16[256,4,2048]{0,2,1:T(8,128)(2,1)} fusion(bf16[256,4,2048]{2,1,0:T(4,128)(2,1)S(1)} %bitcast.47, bf16[1,4,256,256]{3,2,1,0:T(8,128)(2,1)S(1)} %copy-done), kind=kOutput, calls=%fused_computation.12 | convolution fusion | flops 1075838976 | bytes 8912896 | tf_op jit(solution)/shard_map/kjc,jki->ijc/dot_general | solution.py:23
  490.8 8.0 %copy.33 = bf16[256,4,2048]{2,1,0:T(4,128)(2,1)} copy(bf16[256,4,2048]{0,2,1:T(8,128)(2,1)} %convert_bitcast_fusion) | data formatting | bytes 8388608 | tf_op jit(solution)/shard_map/convert_element_type | solution.py:28
  498.8 6.0 all-to-all-start.3
  504.8 0.0 all-reduce.2.cloned.1.call-start
  504.9 0.7 all-reduce.2.cloned.1.call-update
  505.6 103.4 %all-reduce.2.cloned.1.call-done = bf16[1024,2048]{1,0:T(8,128)(2,1)} async-done(((bf16[1024,2048]{1,0:T(8,128)(2,1)}), bf16[1024,2048]{1,0:T(8,128)(2,1)}) %all-reduce.2.cloned.1.call-update) | async-done | bytes 4194320 | tf_op jit(solution)/shard_map/psum | solution.py:15
  609.0 2.3 constant_dynamic-slice_fusion
  611.2 0.0 all-to-all-done.3
  611.2 7.0 %copy.34 = bf16[4,64,4,2048]{3,2,1,0:T(4,128)(2,1)} copy(bf16[4,64,4,2048]{3,2,0,1:T(4,128)(2,1)} %bitcast.21) | data formatting | bytes 8388608 | tf_op jit(solution)/shard_map/all_to_all | solution.py:29
  618.2 6.9 %all_to_all.67 = bf16[4,256,2048]{2,1,0:T(8,128)(2,1)} reshape(bf16[4,64,4,2048]{3,2,1,0:T(4,128)(2,1)} %copy.34) | data formatting | bytes 8388608 | tf_op jit(solution)/shard_map/all_to_all | solution.py:29
  625.2 6.9 %fusion.3 = bf16[4,256,2048]{2,1,0:T(8,128)(2,1)} fusion(bf16[4,256,2048]{2,1,0:T(8,128)(2,1)} %bitcast.43, bf16[4,256,2048]{2,1,0:T(8,128)(2,1)} %all_to_all.67, f32[2048]{0:T(1024)S(1)} %bitcast.54, bf16[1,4,256,256]{3,2,1,0:T(8,128)(2,1)S(1)} %copy-done.2), kind=kOutput, calls=%fused_computation.7 | convolution fusion | flops 1082130432 | bytes 13115392 | tf_op jit(solution)/shard_map/ikc,ikj->ijc/dot_general | solution.py:30
  (1 shorter events, 0.0 us)
Async XLA Ops:
  7.2 124.7 %copy-start = (bf16[1,4,256,256]{3,2,1,0:T(8,128)(2,1)S(1)}, bf16[1,4,256,256]{3,2,1,0:T(8,128)(2,1)}, u32[]{:S(2)}) copy-start(bf16[1,4,256,256]{3,2,1,0:T(8,128)(2,1)} %param.9) | copy-start | bytes 1572868
  147.5 6.9 %copy-start.3 = (bf16[1,2048]{1,0:T(2,128)(2,1)S(1)}, bf16[1,2048]{1,0:T(2,128)(2,1)}, u32[]{:S(2)}) copy-start(bf16[1,2048]{1,0:T(2,128)(2,1)} %param.11) | copy-start | bytes 12292
  147.5 102.0 %all-to-all-start.1 = ((bf16[256,4,2048]{2,1,0:T(4,128)(2,1)}), bf16[256,4,2048]{2,1,0:T(4,128)(2,1)}, u32[]{:S(2)}, u32[]{:S(2)}) async-start(bf16[256,4,2048]{2,1,0:T(4,128)(2,1)} %copy.27), calls=%async_computation.1 | async-start | bytes 8388608 | tf_op jit(solution)/shard_map/all_to_all | solution.py:29
  153.7 119.3 %all-gather.2.cloned.1.call-start = ((), (), s32[]{:S(2)}) async-start(), calls=%async_computation.4 | async-start | bytes 5242880 | tf_op jit(solution)/shard_map/all_gather | solution.py:38
  256.5 7.0 %copy-start.2 = (bf16[1,4,256,256]{3,2,1,0:T(8,128)(2,1)S(1)}, bf16[1,4,256,256]{3,2,1,0:T(8,128)(2,1)}, u32[]{:S(2)}) copy-start(bf16[1,4,256,256]{3,2,1,0:T(8,128)(2,1)} %param.8) | copy-start | bytes 1572868
  270.5 92.5 %collective-permute-start = (bf16[1024,2048]{1,0:T(8,128)(2,1)}, bf16[1024,2048]{1,0:T(8,128)(2,1)}, u32[]{:S(2)}, u32[]{:S(2)}) collective-permute-start(bf16[1024,2048]{1,0:T(8,128)(2,1)} %bitcast.13), channel_id=1, source_target_pairs={{64,0},{128,64},{192,128},{0,192},{65,1},{129,65},{193,129},{1,193... | collective-permute-start | bytes 12582920 | tf_op jit(solution)/shard_map/ppermute | solution.py:10
  366.8 1.9 copy-start.1
  498.8 112.4 %all-to-all-start.3 = ((bf16[256,4,2048]{2,1,0:T(4,128)(2,1)}), bf16[256,4,2048]{2,1,0:T(4,128)(2,1)}, u32[]{:S(2)}, u32[]{:S(2)}) async-start(bf16[256,4,2048]{2,1,0:T(4,128)(2,1)} %copy.33), calls=%async_computation.3 | async-start | bytes 8388608 | tf_op jit(solution)/shard_map/all_to_all | solution.py:29
  504.8 104.1 %all-reduce.2.cloned.1.call-start = ((), (), s32[]{:S(2)}) async-start(), calls=%async_computation.5 | async-start | bytes 8388608 | tf_op jit(solution)/shard_map/psum | solution.py:15
Sparse Core Ops, SparseCore 0:
  156.3 51.5 all-gather.1
  508.6 100.3 all-reduce.1
where the time goes:
time: 645 us; the launch traced here: 639 us
  waiting for transfers between devices  290 us (45%)
  blocking collectives  211 us (33%)
  local copies, waits for them, and re-layouts  71.2 us (11%)
  matrix products  29 us (4%)
  starting transfers between devices  14.7 us (2%)
  between operations  14.4 us (2%)
  other arithmetic  9.1 us (1%)
    all_to_all x2, blocking collectives, mixer(): lax.all_to_all(scaled, 'seq', split_axis=1, concat_axis=0, tiled=True)  211 us
    psum x1, waiting for transfers between devices, from_root(): return lax.psum(jnp.where(mine, array, jnp.zeros_like(array)), axis)  103 us
    all_to_all x2, waiting for transfers between devices, mixer(): lax.all_to_all(mixed, 'seq', split_axis=0, concat_axis=1, tiled=True)  95.1 us
    ppermute x1, waiting for transfers between devices, shifted(): return lax.ppermute(block, axis, route)  90 us
    all_to_all x4, local copies, waits for them, and re-layouts, mixer(): lax.all_to_all(mixed, 'seq', split_axis=0, concat_axis=1, tiled=True)  27.9 us
    all_to_all x2, local copies, waits for them, and re-layouts, mixer(): lax.all_to_all(scaled, 'seq', split_axis=1, concat_axis=0, tiled=True)  16.6 us
    convert_element_type x2, local copies, waits for them, and re-layouts, mixer(): mixed = jnp.einsum('kjc,jki->ijc', lax.all_to_all(scaled, 'seq', split_ax...  15.9 us
    dot_general x2, matrix products, mixer(): jnp.einsum('kjc,jki->ijc', lax.all_to_all(scaled, 'seq', split_axis=1, co...  15.2 us
  transfers between devices with their start and end apart: 5, of which 3 were waited for; matrix products, arithmetic and copies ran while one was open for 3% of the time, Pallas kernels for 0%

commit v1 on v0

--- a/solution.py
+++ b/solution.py
@@ -22,7 +22,10 @@
     scaled = (blocked * inner_part.astype(jnp.float32)).astype(jnp.bfloat16)
     mixed = jnp.einsum(
         "kjc,jki->ijc",
-        lax.all_to_all(scaled, "seq", split_axis=1, concat_axis=0, tiled=True),
+        jnp.concatenate(
+            lax.all_to_all(jnp.stack(jnp.split(scaled, lax.axis_size("seq"), axis=1)), "seq", 0, 0),
+            axis=0,
+        ),
         second_part,
         preferred_element_type=jnp.float32,
     ).astype(jnp.bfloat16)

time: 645 us -> 621 us (0.963)
  local copies, waits for them, and re-layouts: 71.2 us -> 52.4 us
    all_to_all x2 -> x0, local copies, waits for them, and re-layouts: 16.6 us -> none  [mixer(): lax.all_to_all(scaled, 'seq', split_axis=1, concat_axis=0, tiled=True)]
    convert_element_type x4 -> x2, local copies, waits for them, and re-layouts: 22.4 us -> 15.9 us  [mixer(): mixed = jnp.einsum('kjc,jki->ijc', jnp.concatenate(lax.all_to_all(jnp.sta...]
where the time goes in v1:
time: 621 us; the launch traced here: 620 us
  waiting for transfers between devices  290 us (47%)
  blocking collectives  211 us (34%)
  local copies, waits for them, and re-layouts  52.4 us (8%)
  matrix products  28.2 us (5%)
  starting transfers between devices  14.9 us (2%)
  between operations  14.2 us (2%)
  other arithmetic  9.3 us (1%)
    all_to_all x2, blocking collectives, mixer(): lax.all_to_all(jnp.stack(jnp.split(scaled, lax.axis_size('seq'), axis=1))...  211 us
    psum x1, waiting for transfers between devices, from_root(): return lax.psum(jnp.where(mine, array, jnp.zeros_like(array)), axis)  103 us
    all_to_all x2, waiting for transfers between devices, mixer(): lax.all_to_all(mixed, 'seq', split_axis=0, concat_axis=1, tiled=True)  95.1 us
    ppermute x1, waiting for transfers between devices, shifted(): return lax.ppermute(block, axis, route)  90 us
    all_to_all x4, local copies, waits for them, and re-layouts, mixer(): lax.all_to_all(mixed, 'seq', split_axis=0, concat_axis=1, tiled=True)  27.9 us
    convert_element_type x2, local copies, waits for them, and re-layouts, mixer(): mixed = jnp.einsum('kjc,jki->ijc', jnp.concatenate(lax.all_to_all(jnp.sta...  15.9 us
    dot_general x2, matrix products, mixer(): jnp.einsum('kjc,jki->ijc', jnp.concatenate(lax.all_to_all(jnp.stack(jnp.s...  14.3 us
    dot_general x2, matrix products, mixer(): jnp.einsum('ikc,ikj->ijc', returned, first_part, preferred_element_type=j...  13.9 us
  transfers between devices with their start and end apart: 5, of which 3 were waited for; matrix products, arithmetic and copies ran while one was open for 3% of the time, Pallas kernels for 0%

profile of v1, /device:TPU:1, one launch (start us, length us, event | category | flops | bytes accessed | tf_op | source)
XLA Modules:
  0.0 619.6 jit_solution(5609641419897925825)
XLA Ops:
  7.2 0.8 convert_element_type.76
  7.9 3.3 fusion
  11.3 0.1 constant_dynamic-update-slice_fusion.62
  11.4 0.1 constant_dynamic-update-slice_fusion.60
  11.4 0.1 constant_dynamic-update-slice_fusion.58
  11.5 0.1 constant_dynamic-update-slice_fusion.56
  11.6 0.1 constant_dynamic-update-slice_fusion.54
  11.7 0.1 constant_dynamic-update-slice_fusion.52
  11.8 0.1 constant_dynamic-update-slice_fusion.50
  11.9 0.1 constant_dynamic-update-slice_fusion.48
  12.0 0.1 constant_dynamic-update-slice_fusion.46
  12.0 0.1 constant_dynamic-update-slice_fusion.44
  12.1 0.1 constant_dynamic-update-slice_fusion.42
  12.2 0.1 constant_dynamic-update-slice_fusion.40
  12.3 0.1 constant_dynamic-update-slice_fusion.38
  12.4 0.1 constant_dynamic-update-slice_fusion.36
  12.5 0.1 constant_dynamic-update-slice_fusion.34
  12.6 0.1 constant_dynamic-update-slice_fusion.32
  12.6 0.1 constant_dynamic-update-slice_fusion.30
  12.7 0.1 constant_dynamic-update-slice_fusion.28
  12.8 0.1 constant_dynamic-update-slice_fusion.26
  12.9 0.1 constant_dynamic-update-slice_fusion.24
  13.0 0.1 constant_dynamic-update-slice_fusion.22
  13.1 0.1 constant_dynamic-update-slice_fusion.20
  13.1 0.1 constant_dynamic-update-slice_fusion.18
  13.2 0.1 constant_dynamic-update-slice_fusion.16
  13.3 0.1 constant_dynamic-update-slice_fusion.14
  13.4 0.1 constant_dynamic-update-slice_fusion.12
  13.5 0.1 constant_dynamic-update-slice_fusion.10
  13.6 0.1 constant_dynamic-update-slice_fusion.8
  13.7 0.1 constant_dynamic-update-slice_fusion.6
  13.7 0.1 constant_dynamic-update-slice_fusion.4
  13.8 0.1 constant_dynamic-update-slice_fusion.2
  13.9 0.1 constant_dynamic-update-slice_fusion
  14.0 109.1 %all_to_all.46 = bf16[64,4,4,2048]{3,2,1,0:T(4,128)(2,1)S(1)} all-to-all(bf16[64,4,4,2048]{3,2,1,0:T(4,128)(2,1)S(1)} %constant_dynamic-update-slice_fusion), channel_id=1, replica_groups=mesh['pipe'=4,'seq'=64] {'seq'}, dimensions={0} | all-to-all | bytes 8388608 | tf_op jit(solution)/shard_map/all_to_all | solution.py:26
  123.1 7.2 %convert_bitcast_fusion.1 = bf16[256,4,2048]{0,2,1:T(8,128)(2,1)} fusion(bf16[256,4,2048]{2,1,0:T(4,128)(2,1)S(1)} %bitcast.550, bf16[1,4,256,256]{3,2,1,0:T(8,128)(2,1)S(1)} %copy-done), kind=kOutput, calls=%fused_computation.13 | convolution fusion | flops 1075838976 | bytes 8912896 | tf_op jit(solution)/shard_map/kjc,jki->ijc/dot_general | solution.py:23
  130.2 7.9 %copy.23 = bf16[256,4,2048]{2,1,0:T(4,128)(2,1)} copy(bf16[256,4,2048]{0,2,1:T(8,128)(2,1)} %convert_bitcast_fusion.1) | data formatting | bytes 8388608 | tf_op jit(solution)/shard_map/convert_element_type | solution.py:31
  138.2 6.2 all-to-all-start.1
  144.3 0.2 all-gather.2.cloned.1.call-start
  144.5 0.5 all-gather.2.cloned.1.call-update
  145.1 95.1 %all-to-all-done.1 = bf16[256,4,2048]{2,1,0:T(4,128)(2,1)} async-done(((bf16[256,4,2048]{2,1,0:T(4,128)(2,1)}), bf16[256,4,2048]{2,1,0:T(4,128)(2,1)}, u32[]{:S(2)}, u32[]{:S(2)}) %all-to-all-start.1) | async-done | bytes 4194336 | tf_op jit(solution)/shard_map/all_to_all | solution.py:32
  240.2 7.0 %copy.24 = bf16[4,64,4,2048]{3,2,1,0:T(4,128)(2,1)} copy(bf16[4,64,4,2048]{3,2,0,1:T(4,128)(2,1)} %bitcast.72) | data formatting | bytes 8388608 | tf_op jit(solution)/shard_map/all_to_all | solution.py:32
  247.2 7.0 %all_to_all.36 = bf16[4,256,2048]{2,1,0:T(8,128)(2,1)} reshape(bf16[4,64,4,2048]{3,2,1,0:T(4,128)(2,1)} %copy.24) | data formatting | bytes 8388608 | tf_op jit(solution)/shard_map/all_to_all | solution.py:32
  254.2 6.9 %fusion.1 = bf16[4,256,2048]{2,1,0:T(8,128)(2,1)} fusion(bf16[4,256,2048]{2,1,0:T(8,128)(2,1)} %bitcast.553, bf16[4,256,2048]{2,1,0:T(8,128)(2,1)} %all_to_all.36, f32[2048]{0:T(1024)S(1)} %bitcast.557, bf16[1,4,256,256]{3,2,1,0:T(8,128)(2,1)S(1)} %copy-done.2), kind=kOutput, calls=%fused_computation.5 | convolution fusion | flops 1082130432 | bytes 13115392 | tf_op jit(solution)/shard_map/ikc,ikj->ijc/dot_general | solution.py:33
  261.1 2.5 collective-permute-start
  263.6 90.0 %collective-permute-done = bf16[1024,2048]{1,0:T(8,128)(2,1)} collective-permute-done((bf16[1024,2048]{1,0:T(8,128)(2,1)}, bf16[1024,2048]{1,0:T(8,128)(2,1)}, u32[]{:S(2)}, u32[]{:S(2)}) %collective-permute-start) | collective-permute-done | bytes 4194336 | tf_op jit(solution)/shard_map/ppermute | solution.py:10
  353.6 3.9 broadcast_select_fusion
  357.5 1.4 fusion.2
  358.8 1.0 copy-done.1
  359.8 0.1 constant_dynamic-update-slice_fusion.126
  359.9 0.1 constant_dynamic-update-slice_fusion.124
  360.0 0.1 constant_dynamic-update-slice_fusion.122
  360.1 0.1 constant_dynamic-update-slice_fusion.120
  360.2 0.1 constant_dynamic-update-slice_fusion.118
  362.5 101.9 %all_to_all.47 = bf16[64,4,4,2048]{3,2,1,0:T(4,128)(2,1)S(1)} all-to-all(bf16[64,4,4,2048]{3,2,1,0:T(4,128)(2,1)S(1)} %constant_dynamic-update-slice_fusion.64), channel_id=1, replica_groups=mesh['pipe'=4,'seq'=64] {'seq'}, dimensions={0} | all-to-all | bytes 8388608 | tf_op jit(solution)/shard_map/all_to_all | solution.py:26
  464.4 7.1 %convert_bitcast_fusion = bf16[256,4,2048]{0,2,1:T(8,128)(2,1)} fusion(bf16[256,4,2048]{2,1,0:T(4,128)(2,1)S(1)} %bitcast.551, bf16[1,4,256,256]{3,2,1,0:T(8,128)(2,1)S(1)} %copy-done), kind=kOutput, calls=%fused_computation.12 | convolution fusion | flops 1075838976 | bytes 8912896 | tf_op jit(solution)/shard_map/kjc,jki->ijc/dot_general | solution.py:23
  471.5 8.0 %copy.27 = bf16[256,4,2048]{2,1,0:T(4,128)(2,1)} copy(bf16[256,4,2048]{0,2,1:T(8,128)(2,1)} %convert_bitcast_fusion) | data formatting | bytes 8388608 | tf_op jit(solution)/shard_map/convert_element_type | solution.py:31
  479.5 6.0 all-to-all-start.3
  485.6 0.7 all-reduce.2.cloned.1.call-update
  486.3 103.4 %all-reduce.2.cloned.1.call-done = bf16[1024,2048]{1,0:T(8,128)(2,1)} async-done(((bf16[1024,2048]{1,0:T(8,128)(2,1)}), bf16[1024,2048]{1,0:T(8,128)(2,1)}) %all-reduce.2.cloned.1.call-update) | async-done | bytes 4194320 | tf_op jit(solution)/shard_map/psum | solution.py:15
  589.7 2.3 constant_dynamic-slice_fusion
  591.9 7.0 %copy.28 = bf16[4,64,4,2048]{3,2,1,0:T(4,128)(2,1)} copy(bf16[4,64,4,2048]{3,2,0,1:T(4,128)(2,1)} %bitcast.145) | data formatting | bytes 8388608 | tf_op jit(solution)/shard_map/all_to_all | solution.py:32
  598.9 6.9 %all_to_all.41 = bf16[4,256,2048]{2,1,0:T(8,128)(2,1)} reshape(bf16[4,64,4,2048]{3,2,1,0:T(4,128)(2,1)} %copy.28) | data formatting | bytes 8388608 | tf_op jit(solution)/shard_map/all_to_all | solution.py:32
  605.9 6.9 %fusion.3 = bf16[4,256,2048]{2,1,0:T(8,128)(2,1)} fusion(bf16[4,256,2048]{2,1,0:T(8,128)(2,1)} %bitcast.549, bf16[4,256,2048]{2,1,0:T(8,128)(2,1)} %all_to_all.41, f32[2048]{0:T(1024)S(1)} %bitcast.558, bf16[1,4,256,256]{3,2,1,0:T(8,128)(2,1)S(1)} %copy-done.2), kind=kOutput, calls=%fused_computation.7 | convolution fusion | flops 1082130432 | bytes 13115392 | tf_op jit(solution)/shard_map/ikc,ikj->ijc/dot_general | solution.py:33
  (102 shorter events, 3.6 us)
Async XLA Ops:
  7.2 115.9 %copy-start = (bf16[1,4,256,256]{3,2,1,0:T(8,128)(2,1)S(1)}, bf16[1,4,256,256]{3,2,1,0:T(8,128)(2,1)}, u32[]{:S(2)}) copy-start(bf16[1,4,256,256]{3,2,1,0:T(8,128)(2,1)} %param.9) | copy-start | bytes 1572868
  138.2 6.9 %copy-start.3 = (bf16[1,2048]{1,0:T(2,128)(2,1)S(1)}, bf16[1,2048]{1,0:T(2,128)(2,1)}, u32[]{:S(2)}) copy-start(bf16[1,2048]{1,0:T(2,128)(2,1)} %param.11) | copy-start | bytes 12292
  138.2 102.0 %all-to-all-start.1 = ((bf16[256,4,2048]{2,1,0:T(4,128)(2,1)}), bf16[256,4,2048]{2,1,0:T(4,128)(2,1)}, u32[]{:S(2)}, u32[]{:S(2)}) async-start(bf16[256,4,2048]{2,1,0:T(4,128)(2,1)} %copy.23), calls=%async_computation.1 | async-start | bytes 8388608 | tf_op jit(solution)/shard_map/all_to_all | solution.py:32
  144.3 119.3 %all-gather.2.cloned.1.call-start = ((), (), s32[]{:S(2)}) async-start(), calls=%async_computation.4 | async-start | bytes 5242880 | tf_op jit(solution)/shard_map/all_gather | solution.py:41
  247.2 7.0 %copy-start.2 = (bf16[1,4,256,256]{3,2,1,0:T(8,128)(2,1)S(1)}, bf16[1,4,256,256]{3,2,1,0:T(8,128)(2,1)}, u32[]{:S(2)}) copy-start(bf16[1,4,256,256]{3,2,1,0:T(8,128)(2,1)} %param.8) | copy-start | bytes 1572868
  261.1 92.5 %collective-permute-start = (bf16[1024,2048]{1,0:T(8,128)(2,1)}, bf16[1024,2048]{1,0:T(8,128)(2,1)}, u32[]{:S(2)}, u32[]{:S(2)}) collective-permute-start(bf16[1024,2048]{1,0:T(8,128)(2,1)} %bitcast.75), channel_id=1, source_target_pairs={{64,0},{128,64},{192,128},{0,192},{65,1},{129,65},{193,129},{1,193... | collective-permute-start | bytes 12582920 | tf_op jit(solution)/shard_map/ppermute | solution.py:10
  357.5 2.3 copy-start.1
  479.5 112.4 %all-to-all-start.3 = ((bf16[256,4,2048]{2,1,0:T(4,128)(2,1)}), bf16[256,4,2048]{2,1,0:T(4,128)(2,1)}, u32[]{:S(2)}, u32[]{:S(2)}) async-start(bf16[256,4,2048]{2,1,0:T(4,128)(2,1)} %copy.27), calls=%async_computation.3 | async-start | bytes 8388608 | tf_op jit(solution)/shard_map/all_to_all | solution.py:32
  485.5 104.1 %all-reduce.2.cloned.1.call-start = ((), (), s32[]{:S(2)}) async-start(), calls=%async_computation.5 | async-start | bytes 8388608 | tf_op jit(solution)/shard_map/psum | solution.py:15
Sparse Core Ops, SparseCore 0:
  146.9 51.5 all-gather.1
  489.3 100.3 all-reduce.1
